TPU v7x, 256 devices: a whole 4x4x8 slice. The times are simulated.
256 devices in a mesh: corpus: 64 (over y, z, x_hi), vocab: 4 (over x_lo, core).
Axes of the slice: x: 4 (x_hi: 2, x_lo: 2; x = x_hi * 2 + x_lo), y: 4, z: 8, core: 2. Of those that a mesh axis runs over, the one named last changes fastest.
Arguments:
- eval_tiles: bfloat16 [64, 12, 128, 512], P('corpus', 'vocab'), may hold values from 0.019897461 to 2
- eval_tile_list: int32 [64, 12], P(None, 'vocab'), may hold values from 0 to 128, as said below
- corpus_tiles: bfloat16 [256, 12, 128, 512], P('corpus', 'vocab'), may hold values from 0.019897461 to 2
- corpus_tile_list: int32 [256, 12], P('corpus', 'vocab'), may hold values from 0 to 128, as said below
- pair_eval_block: int32 [6144], P('corpus'), may hold values from 0 to 63
- pair_corpus_block: int32 [6144], P('corpus'), may hold values from 0 to 3
- pair_count: int32 [64], P('corpus'), may hold values from 12 to 96, as said below
- eval_norm: float32 [8192], replicated, may hold values from 8 to 32
- corpus_norm: float32 [32768], P('corpus'), may hold values from 8 to 32
Outputs:
- cosine_tiles: float32 [6144, 128, 128], P(('corpus', 'vocab'))
Inputs may be any that keep to these rules, and one draw needn't show every extreme that they name: `eval_tile_list`: value 128 marks an empty slot; other ids of one row block in one slice are distinct. Slot 0 of a block and slice is never empty. `corpus_tile_list`: value 128 marks an empty slot; other ids of one row block in one slice are distinct. Slot 0 of a block and slice is never empty. Shard c's live pair slots are its first pair_count[c] slots. Some shard is full.
All inputs are finite; a program needn't handle non-finite values.
Results may differ from a plain program's by a relative error of at most 0.0003.
Values may be sent and summed in bfloat16 or wider, within the bound.
A program may use at most 128 MiB of HBM per device.

v0:
```python
import jax
import jax.numpy as jnp
from jax import lax
from jax.sharding import PartitionSpec as P

VOCAB = 262144
GROUP = 8


def local(
    eval_tiles,
    eval_tile_list,
    corpus_tiles,
    corpus_tile_list,
    pair_eval_block,
    pair_corpus_block,
    pair_count,
    eval_norm,
    corpus_norm,
):
    slices = lax.axis_size("vocab")
    term_width = corpus_tiles.shape[3]
    tile_rows = corpus_tiles.shape[2]
    tiles_slice = VOCAB // (term_width * slices)
    pair_slots = pair_eval_block.shape[0]
    quarter = pair_slots // slices
    every_eval = lax.all_gather(eval_tiles, "corpus", axis=0, tiled=True)
    position = jnp.arange(pair_slots, dtype=jnp.int32)
    own_live = position < pair_count[0]
    groups = quarter * lax.axis_size("vocab") // GROUP

    def one_group(group_index, totals):
        first_slot = group_index * GROUP
        living = lax.dynamic_slice_in_dim(own_live, first_slot, GROUP)

        def compute(current):
            eval_index = lax.dynamic_slice_in_dim(pair_eval_block, first_slot, GROUP)
            block_index = lax.dynamic_slice_in_dim(pair_corpus_block, first_slot, GROUP)
            eval_part = every_eval[eval_index]
            eval_list = eval_tile_list[eval_index]
            corpus_part = corpus_tiles[block_index]
            corpus_list = corpus_tile_list[block_index]
            matched = (eval_list[:, :, None] == corpus_list[:, None, :]) & (
                eval_list[:, :, None] < tiles_slice
            )
            aligned = jnp.einsum(
                "gij,gjrt->girt",
                matched.astype(jnp.bfloat16),
                corpus_part,
                preferred_element_type=jnp.float32,
            ).astype(jnp.bfloat16)
            products = jnp.einsum(
                "girt,gist->grs", eval_part, aligned, preferred_element_type=jnp.float32
            )
            products = jnp.where(living[:, None, None], products, 0.0)
            return lax.dynamic_update_slice_in_dim(current, products, group_index * GROUP, 0)

        return lax.cond(jnp.any(living), compute, lambda current: current, totals)

    start_totals = jnp.zeros((quarter * lax.axis_size("vocab"), tile_rows, tile_rows), jnp.float32)
    summed = lax.psum_scatter(
        lax.fori_loop(0, groups, one_group, start_totals), "vocab", scatter_dimension=0, tiled=True
    )
    vocab_index = lax.axis_index("vocab")
    first_pair = vocab_index * quarter
    mine_eval = lax.dynamic_slice_in_dim(pair_eval_block, first_pair, quarter)
    mine_block = lax.dynamic_slice_in_dim(pair_corpus_block, first_pair, quarter)
    mine_live = lax.dynamic_slice_in_dim(own_live, first_pair, quarter)
    eval_scale = eval_norm.reshape(-1, tile_rows)[mine_eval]
    corpus_scale = corpus_norm.reshape(-1, tile_rows)[mine_block]
    cosine = summed / (eval_scale[:, :, None] * corpus_scale[:, None, :])
    return jnp.where(mine_live[:, None, None], cosine, 0.0)


def solution(mesh):
    in_specs = (
        P("corpus", "vocab", None, None),
        P(None, "vocab"),
        P("corpus", "vocab", None, None),
        P("corpus", "vocab"),
        P("corpus"),
        P("corpus"),
        P("corpus"),
        P(),
        P("corpus"),
    )
    out_specs = P(("corpus", "vocab"), None, None)
    return jax.shard_map(local, mesh=mesh, in_specs=in_specs, out_specs=out_specs, check_vma=False)
```

profile of v0, /device:TPU:33, one launch (start us, length us, event | category | flops | bytes accessed | tf_op | source)
XLA Modules:
  0.0 634.8 jit_solution(17635871114623681145)
XLA Ops:
  6.5 0.7 all-gather.2.cloned.1.call-update
  7.3 0.0 reduce-scatter.2.cloned.1.call-start
  8.0 0.8 copy.11
  8.7 0.0 copy-start.3
  8.7 0.0 copy-start.5
  8.8 0.0 copy-start.6
  8.8 276.1 %all-gather.2.cloned.1.call-done = bf16[64,3,128,512]{3,2,1,0:T(8,128)(2,1)} async-done(((bf16[1,3,128,512]{3,2,1,0:T(8,128)(2,1)}), bf16[64,3,128,512]{3,2,1,0:T(8,128)(2,1)}) %all-gather.2.cloned.1.call-update) | async-done | bytes 25165840 | tf_op jit(solution)/shard_map/all_gather | solution.py:27
  284.9 3.5 broadcast_in_dim.49
  288.3 0.0 copy-done.5
  288.3 60.8 %while.16 = (s32[]{:T(128)}, f32[96,128,128]{2,1,0:T(8,128)}, pred[96]{0:T(512)(128)(4,1)S(1)}, s32[96]{0:T(128)S(1)}, bf16[64,3,128,512]{3,2,1,0:T(8,128)(2,1)}...) while((s32[]{:T(128)}, f32[96,128,128]{2,1,0:T(8,128)}, ...), condition=%wide.region_4.5_spmd, body=%wide.region_0.4_spmd.sunk | while | flops 412223712 | bytes 38282672 | solution.py:62
  288.4 0.8 fusion.15
  289.8 21.3 %conditional.2 = (f32[96,128,128]{2,1,0:T(8,128)}) conditional(s32[]{:T(128)} %convert_element_type.20, f32[96,128,128]{2,1,0:T(8,128)} %get-tuple-element.313, (pred[8]{0:T(512)(128)(4,1)S(1)}, s32[]{:T(128)}, s32[96]{0:T(128)S(1)}, bf16[64,3,128,512]{3,2,1,0:T(8,128)(2,1)}, s32[64,3]{1,0:T(8,128)S(1)}, /*index=5*/s32[96]{0:T(128)S(1)}, ...), branch_computations={%region_2.0_spmd, %region_3.3_spmd} | conditional | flops 412223712 | bytes 38282388 | solution.py:58
  289.9 0.1 compare_select_fusion
  290.0 10.5 %gather_fusion = bf16[8,3,128,512]{3,2,1,0:T(8,128)(2,1)} fusion(bf16[64,3,128,512]{3,2,1,0:T(8,128)(2,1)} %get-tuple-element.178, s32[1024]{0:T(1024)S(1)} %pad_clamp_fusion.1), kind=kCustom, calls=%fused_computation | custom fusion | bytes 6291488 | tf_op jit(solution)/shard_map/while/body/eval_jaxpr/cond/branch_1_fun/gather | solution.py:39
  300.5 2.5 gather_fusion.3
  303.0 0.6 gather_fusion.2
  303.6 0.6 gather_fusion.1
  304.1 0.0 copy-start.2
  304.1 4.9 fusion
  309.1 2.1 fusion.5
  311.2 0.8 fusion.15
  312.6 21.3 %conditional.2 = (f32[96,128,128]{2,1,0:T(8,128)}) conditional(s32[]{:T(128)} %convert_element_type.20, f32[96,128,128]{2,1,0:T(8,128)} %get-tuple-element.313, (pred[8]{0:T(512)(128)(4,1)S(1)}, s32[]{:T(128)}, s32[96]{0:T(128)S(1)}, bf16[64,3,128,512]{3,2,1,0:T(8,128)(2,1)}, s32[64,3]{1,0:T(8,128)S(1)}, /*index=5*/s32[96]{0:T(128)S(1)}, ...), branch_computations={%region_2.0_spmd, %region_3.3_spmd} | conditional | flops 412223712 | bytes 38282388 | solution.py:58
  312.7 0.1 compare_select_fusion
  312.8 10.5 %gather_fusion = bf16[8,3,128,512]{3,2,1,0:T(8,128)(2,1)} fusion(bf16[64,3,128,512]{3,2,1,0:T(8,128)(2,1)} %get-tuple-element.178, s32[1024]{0:T(1024)S(1)} %pad_clamp_fusion.1), kind=kCustom, calls=%fused_computation | custom fusion | bytes 6291488 | tf_op jit(solution)/shard_map/while/body/eval_jaxpr/cond/branch_1_fun/gather | solution.py:39
  323.3 2.5 gather_fusion.3
  325.8 0.6 gather_fusion.2
  326.4 0.6 gather_fusion.1
  326.9 4.9 fusion
  331.9 2.1 fusion.5
  334.0 0.8 fusion.15
  335.5 0.8 fusion.15
  337.0 0.8 fusion.15
  338.5 0.8 fusion.15
  340.1 0.8 fusion.15
  341.6 0.8 fusion.15
  343.1 0.8 fusion.15
  344.6 0.8 fusion.15
  346.1 0.8 fusion.15
  347.7 0.8 fusion.15
  349.2 0.0 copy-start.4
  349.2 0.0 reduce-scatter.2.cloned.1.call-update
  349.2 0.1 dynamic_slice.22
  349.3 0.1 compare_select_fusion.2
  349.4 0.5 copy-done.4
  349.9 0.6 gather_fusion.5
  350.5 0.6 gather_fusion.4
  351.0 273.8 %reduce-scatter.2.cloned.1.call-done = f32[24,128,128]{2,1,0:T(8,128)} async-done(((f32[96,128,128]{2,1,0:T(8,128)}), f32[24,128,128]{2,1,0:T(8,128)}) %reduce-scatter.2.cloned.1.call-update) | async-done | bytes 1572880 | tf_op jit(solution)/shard_map/reduce_scatter | solution.py:61
  624.9 3.1 divide_select_fusion
  (29 shorter events, 0.2 us)
Async XLA Ops:
  6.5 343.9 %copy-start = (f32[8192]{0:T(1024)S(1)}, f32[8192]{0:T(1024)}, u32[]{:S(2)}) copy-start(f32[8192]{0:T(1024)} %param.20) | copy-start | bytes 98308
  6.5 278.3 %all-gather.2.cloned.1.call-start = ((), (), s32[]{:S(2)}) async-start(), calls=%async_computation.1 | async-start | bytes 25559040 | tf_op jit(solution)/shard_map/all_gather | solution.py:27
  7.3 617.6 %reduce-scatter.2.cloned.1.call-start = ((), (), s32[]{:S(2)}) async-start(), calls=%async_computation.2 | async-start | bytes 7864320 | tf_op jit(solution)/shard_map/reduce_scatter | solution.py:61
  8.7 279.6 %copy-start.1 = (bf16[4,3,128,512]{3,2,1,0:T(8,128)(2,1)S(1)}, bf16[4,3,128,512]{3,2,1,0:T(8,128)(2,1)}, u32[]{:S(2)}) copy-start(bf16[4,3,128,512]{3,2,1,0:T(8,128)(2,1)} %param.15) | copy-start | bytes 4718596
  8.7 279.6 %copy-start.3 = (s32[4,3]{1,0:T(4,128)S(1)}, s32[4,3]{1,0:T(4,128)}, u32[]{:S(2)}) copy-start(s32[4,3]{1,0:T(4,128)} %param.16) | copy-start | bytes 148
  8.7 279.6 %copy-start.5 = (s32[96]{0:T(128)S(1)}, s32[96]{0:T(128)}, u32[]{:S(2)}) copy-start(s32[96]{0:T(128)} %param.17) | copy-start | bytes 1156
  8.8 279.6 %copy-start.6 = (s32[96]{0:T(128)S(1)}, s32[96]{0:T(128)}, u32[]{:S(2)}) copy-start(s32[96]{0:T(128)} %param.18) | copy-start | bytes 1156
  304.1 4.9 copy-start.2
  326.9 4.9 copy-start.2
  349.2 0.7 copy-start.4
Sparse Core Ops, SparseCore 0:
  11.0 273.8 all-gather.1
  349.3 275.4 reduce-scatter.1
where the time goes:
time: 637 us; the launch traced here: 635 us
  waiting for transfers between devices  551 us (86%)
  local copies, waits for them, and re-layouts  34.3 us (5%)
  between operations  14.1 us (2%)
  matrix products  14 us (2%)
  other arithmetic  12.8 us (2%)
  loops' own time  8.9 us (1%)
    all_gather x1, waiting for transfers between devices, local(): every_eval = lax.all_gather(eval_tiles, 'corpus', axis=0, tiled=True)  276 us
    reduce_scatter x1, waiting for transfers between devices, local(): lax.psum_scatter(lax.fori_loop(0, groups, one_group, start_totals), 'voca...  274 us
    gather x2, local copies, waits for them, and re-layouts, compute(): eval_part = every_eval[eval_index]  21.1 us
  transfers between devices with their start and end apart: 2, of which 2 were waited for; matrix products, arithmetic and copies ran while one was open for 0% of the time, Pallas kernels for 0%

commit v1 on v0

v1 whole, which is shorter than its diff:
```python
import functools
import heapq

import jax
import jax.numpy as jnp
from jax import lax
from jax.experimental import pallas as pl
from jax.experimental.pallas import tpu as pltpu
from jax.sharding import PartitionSpec as P

MESH = pl.DeviceIdType.MESH
VOCAB = 262144
NZ = 8
CHUNK = 6


def place(ny):
    c = lax.axis_index("corpus")
    v = lax.axis_index("vocab")
    h = lax.rem(c, 2)
    t = lax.div(c, 2)
    return lax.div(t, NZ), lax.rem(t, NZ), h, lax.div(v, 2), lax.rem(v, 2)


def device(y, z, h, lo, core):
    return ((y * NZ + z) * 2 + h, lo * 2 + core)


def along_x(h, lo, step):
    x = lax.rem(h * 2 + lo + step + 4, 4)
    return lax.div(x, 2), lax.rem(x, 2)


def plane_order(ny, nz, a, b):
    messages = {}
    for colour, n1, n2, rows, l1, l2 in (("A", nz, ny, a, "z", "y"), ("B", ny, nz, b, "y", "z")):
        for sign in (1, -1):
            for s in range(n1 - 1):
                before = (colour, sign, s - 1, -1) if s else None
                messages[colour, sign, s, -1] = (l1, sign, rows, before)
            for s in range(n1):
                for t in range(n2 - 1):
                    if t:
                        before = (colour, sign, s, t - 1)
                    else:
                        before = (colour, sign, s - 1, -1) if s else None
                    messages[colour, sign, s, t] = (l2, sign, rows, before)
    after = {}
    for key, (_, _, _, before) in messages.items():
        after.setdefault(before, []).append(key)

    def rank(key):
        return -100 if key[3] < 0 else key[3]

    free = {}
    heap = []
    count = 0

    def issue(key, now):
        nonlocal count
        axis, sign, rows, _ = messages[key]
        end = max(now, free.get((axis, sign), 0.0)) + rows * 1.024 / 46.5
        free[axis, sign] = end
        count += 1
        heapq.heappush(heap, (end + 1.8, count, key))

    first = sorted(after[None], key=rank)
    for key in first:
        issue(key, 0.0)
    events = []
    while heap:
        now, _, key = heapq.heappop(heap)
        follow = sorted(after.get(key, []), key=rank)
        for nxt in follow:
            issue(nxt, now)
        events.append((key, follow))
    return messages, first, events


def gather_kernel(
    ny, rows_a, eval_in, corpus_in, meta_in, gath, pcorpus, relay, pmeta,
    bounce, send, recv, xsend, xrecv, local_sem,
):
    nz = NZ
    rows = eval_in.shape[0]
    rows_b = rows // 2 - rows_a
    y, z, h, lo, core = place(ny)
    up_y = device(lax.rem(y + 1, ny), z, h, lo, core)
    down_y = device(lax.rem(y + ny - 1, ny), z, h, lo, core)
    up_z = device(y, lax.rem(z + 1, nz), h, lo, core)
    down_z = device(y, lax.rem(z + nz - 1, nz), h, lo, core)
    up_x = device(y, z, *along_x(h, lo, 1), core)
    down_x = device(y, z, *along_x(h, lo, -1), core)
    partner = device(y, z, 1 - h, lo, core)
    targets = {("y", 1): up_y, ("y", -1): down_y, ("z", 1): up_z, ("z", -1): down_z}

    barrier = pltpu.get_barrier_semaphore()
    peers = (up_y, down_y, up_z, down_z, up_x, down_x, partner)
    for peer in peers:
        pl.semaphore_signal(barrier, inc=1, device_id=peer, device_id_type=MESH)
    pl.semaphore_wait(barrier, len(peers))

    messages, first, events = plane_order(ny, nz, rows_a, rows_b)
    number = {key: i for i, key in enumerate(messages)}
    start_row = {("A", 1): 0, ("A", -1): rows_a, ("B", 1): 2 * rows_a, ("B", -1): 2 * rows_a + rows_b}

    def copy(key):
        colour, sign, s, t = key
        axis, _, size, before = messages[key]
        span = pl.ds(start_row[colour, sign], size)
        if t < 0:
            back1, back2 = s, 0
        else:
            back1, back2 = s, t
        if colour == "A":
            oz, oy = z - sign * back1, y - sign * back2
        else:
            oy, oz = y - sign * back1, z - sign * back2
        slot = lax.rem(oy + ny, ny) * nz + lax.rem(oz + nz, nz)
        src = eval_in.at[span] if before is None else gath.at[slot, span]
        i = number[key]
        return pltpu.make_async_remote_copy(
            src_ref=src, dst_ref=gath.at[slot, span], send_sem=send.at[i], recv_sem=recv.at[i],
            device_id=targets[axis, sign], device_id_type=MESH,
        )

    for key in first:
        copy(key).start()

    half = corpus_in.shape[0] // 2
    low, high = pl.ds(0, half), pl.ds(half, half)

    def xcopy(i, src, dst, target):
        return pltpu.make_async_remote_copy(
            src_ref=src, dst_ref=dst, send_sem=xsend.at[i], recv_sem=xrecv.at[i],
            device_id=target, device_id_type=MESH,
        )

    hop1 = [
        xcopy(0, corpus_in.at[low], relay.at[low], up_x),
        xcopy(1, corpus_in.at[high], relay.at[high], down_x),
    ]
    hop2 = [
        xcopy(2, relay.at[low], pcorpus.at[low], up_x),
        xcopy(3, relay.at[high], pcorpus.at[high], down_x),
    ]
    lists = xcopy(4, meta_in, pmeta, partner)
    lists.start()
    for c in hop1:
        c.start()
    own_slot = y * nz + z
    into = pltpu.make_async_copy(eval_in, bounce, local_sem)
    into.start()
    into.wait()
    back = pltpu.make_async_copy(bounce, gath.at[own_slot], local_sem)
    back.start()

    relay_after = len(events) // 4
    for n, (key, follow) in enumerate(events):
        if n == relay_after:
            for c, d in zip(hop1, hop2):
                c.wait_recv()
                d.start()
        copy(key).wait_recv()
        for nxt in follow:
            copy(nxt).start()
    back.wait()
    lists.wait()
    for c in hop2:
        c.wait()
    for c in hop1:
        c.wait_send()
    for key in messages:
        copy(key).wait_send()


def gather(ny, rows_a, eval_in, corpus_in, meta):
    n = len(plane_order(ny, NZ, 1, 1)[0])
    return pl.pallas_call(
        functools.partial(gather_kernel, ny, rows_a),
        name="plane_gather",
        out_shape=(
            jax.ShapeDtypeStruct((ny * NZ,) + eval_in.shape, eval_in.dtype),
            jax.ShapeDtypeStruct(corpus_in.shape, corpus_in.dtype),
            jax.ShapeDtypeStruct(corpus_in.shape, corpus_in.dtype),
            jax.ShapeDtypeStruct(meta.shape, meta.dtype),
        ),
        in_specs=[pl.BlockSpec(memory_space=pl.ANY)] * 3,
        out_specs=[pl.BlockSpec(memory_space=pl.ANY)] * 4,
        scratch_shapes=[
            pltpu.VMEM(eval_in.shape, eval_in.dtype),
            pltpu.SemaphoreType.DMA((n,)),
            pltpu.SemaphoreType.DMA((n,)),
            pltpu.SemaphoreType.DMA((5,)),
            pltpu.SemaphoreType.DMA((5,)),
            pltpu.SemaphoreType.DMA,
        ],
        compiler_params=pltpu.CompilerParams(collective_id=0, has_side_effects=True),
    )(eval_in, corpus_in, meta)


def dot_kernel(
    pairs, docs, slots, tiles_slice, meta, pmeta, lists, gath, corpus, pcorpus, part,
    evals, texts, table, codes, ring, zero, load_sem, out_sem,
):
    nb, rows, _ = gath.shape
    tile = rows // slots
    h = lax.rem(lax.axis_index("corpus"), 2)
    loads = [
        pltpu.make_async_copy(gath, evals, load_sem.at[0]),
        pltpu.make_async_copy(corpus, texts.at[0], load_sem.at[1]),
        pltpu.make_async_copy(pcorpus, texts.at[1], load_sem.at[2]),
    ]
    for c in loads:
        c.start()
    zero[...] = jnp.zeros_like(zero)

    def read(shard, i):
        return (meta, pmeta)[shard][i // 128, i % 128]

    width = lists.shape[1]
    for shard in range(2):
        for k in range(docs):
            code = jnp.zeros((1, width), jnp.int32)
            for i in range(slots):
                ids = lists[i : i + 1, :]
                hit = jnp.zeros((1, width), jnp.int32)
                for j in range(slots):
                    own = read(shard, 2 * pairs + k * slots + j)
                    hit = jnp.where(ids == own, j + 1, hit)
                code += jnp.where(ids < tiles_slice, hit, 0) * (4**i)
            table[shard * docs + k : shard * docs + k + 1, 0:width] = code
    send = pltpu.make_async_copy(table, codes, load_sem.at[3])
    send.start()
    send.wait()
    for c in loads:
        c.wait()

    depth = ring.shape[0]
    for shard in range(2):
        lists_of = (meta, pmeta)[shard]
        at = 2 * pairs + docs * slots
        count = lists_of[at // 128, at % 128]

        def one_pair(p, _, shard=shard, lists_of=lists_of, count=count):
            e = lists_of[lax.div(p, 128), lax.rem(p, 128)]
            q = p + pairs
            k = lists_of[lax.div(q, 128), lax.rem(q, 128)]
            code = codes[shard * docs + k, e]
            live = (p < count) & (lax.rem(e, 2) == h) & (code > 0)
            n = lax.rem(p, depth)

            @pl.when(jnp.logical_or(p >= depth, shard > 0))
            def _():
                pltpu.make_async_copy(ring.at[0], part.at[0, 0], out_sem.at[n]).wait()

            @pl.when(jnp.logical_not(live))
            def _():
                pltpu.make_async_copy(zero, part.at[shard, p], out_sem.at[n]).start()

            @pl.when(live)
            def _():
                ring[n] = jnp.zeros(ring.shape[1:], jnp.float32)
                block = lax.div(e, 2)
                for i in range(slots):
                    j = lax.rem(lax.div(code, 4**i), 4)

                    @pl.when(j > 0)
                    def _():
                        first = pl.multiple_of((k * slots + j - 1) * tile, tile)
                        ring[n] += lax.dot_general(
                            evals[block, pl.ds(i * tile, tile), :],
                            texts[shard, pl.ds(first, tile), :],
                            (((1,), (1,)), ((), ())),
                            preferred_element_type=jnp.float32,
                        )

                pltpu.make_async_copy(ring.at[n], part.at[shard, p], out_sem.at[n]).start()

            return 0

        lax.fori_loop(0, pairs, one_pair, 0)
    for n in range(depth):
        pltpu.make_async_copy(ring.at[0], part.at[0, 0], out_sem.at[n]).wait()


def partial_dots(pairs, docs, slots, tiles_slice, meta, pmeta, lists, gath, corpus, pcorpus):
    tile = gath.shape[1] // slots
    smem = pl.BlockSpec(memory_space=pltpu.SMEM)
    anyspace = pl.BlockSpec(memory_space=pl.ANY)
    return pl.pallas_call(
        functools.partial(dot_kernel, pairs, docs, slots, tiles_slice),
        name="partial_dots",
        out_shape=jax.ShapeDtypeStruct((2, pairs, tile, tile), jnp.float32),
        in_specs=[smem, smem, pl.BlockSpec(memory_space=pltpu.VMEM), anyspace, anyspace, anyspace],
        out_specs=anyspace,
        scratch_shapes=[
            pltpu.VMEM(gath.shape, gath.dtype),
            pltpu.VMEM((2,) + corpus.shape, corpus.dtype),
            pltpu.VMEM((8, 128), jnp.int32),
            pltpu.SMEM((8, 128), jnp.int32),
            pltpu.VMEM((8, tile, tile), jnp.float32),
            pltpu.VMEM((tile, tile), jnp.float32),
            pltpu.SemaphoreType.DMA((4,)),
            pltpu.SemaphoreType.DMA((8,)),
        ],
    )(meta, pmeta, lists, gath, corpus, pcorpus)


def reduce_kernel(
    ny, quarter, part, out, own, sib, outq, outs, inq, ins,
    lsem, dsend, drecv, qsend, qrecv, ssend, srecv,
):
    half = quarter // 2
    y, z, h, lo, core = place(ny)
    up = device(y, z, *along_x(h, lo, 1), core)
    down = device(y, z, *along_x(h, lo, -1), core)
    sibling = device(y, z, h, lo, 1 - core)
    barrier = pltpu.get_barrier_semaphore()
    for peer in (up, down, sibling):
        pl.semaphore_signal(barrier, inc=1, device_id=peer, device_id_type=MESH)
    pl.semaphore_wait(barrier, 3)

    def chunk_list(step, begin):
        return [(step % 4, begin + k, min(CHUNK, half - k)) for k in range(0, half, CHUNK)]

    groups = [
        (0, "far", chunk_list(2, 0)),
        (1, "far", chunk_list(2, half)),
        (0, "near", chunk_list(1, half)),
        (1, "near", chunk_list(-1, 0)),
        (0, "join", chunk_list(1, 0)),
        (1, "join", chunk_list(-1, half)),
        (2, "mine", chunk_list(0, 0)),
        (3, "mine", chunk_list(0, half)),
    ]
    steps = len(groups[0][2])
    order = []
    for pair in range(0, len(groups), 2):
        for s in range(steps):
            for g in (pair, pair + 1):
                order.append((g, s))
    loads = {}
    for i, (g, s) in enumerate(order):
        step, begin, size = groups[g][2][s]
        hx, lx = along_x(h, lo, step)
        shard = lax.rem(hx + h, 2)
        mine = (lx * 2 + core) * quarter + begin
        theirs = (lx * 2 + 1 - core) * quarter + begin
        span = pl.ds(begin, size)
        a = pltpu.make_async_copy(
            part.at[shard, pl.ds(mine, size)], own.at[step, span], lsem.at[i]
        )
        b = pltpu.make_async_remote_copy(
            src_ref=part.at[shard, pl.ds(theirs, size)], dst_ref=sib.at[step, span],
            send_sem=dsend.at[i], recv_sem=drecv.at[i], device_id=sibling, device_id_type=MESH,
        )
        a.start()
        b.start()
        loads[g, s] = (a, b)

    stage = {"far": 0, "near": 1, "join": 2}
    sends = []

    def message(way, kind, s):
        n = (way * 3 + stage[kind]) * steps + s
        span = pl.ds(n * CHUNK, CHUNK)
        target = up if way == 0 else down
        q = pltpu.make_async_remote_copy(
            src_ref=outq.at[span], dst_ref=inq.at[span], send_sem=qsend.at[n],
            recv_sem=qrecv.at[n], device_id=target, device_id_type=MESH,
        )
        t = pltpu.make_async_remote_copy(
            src_ref=outs.at[n], dst_ref=ins.at[n], send_sem=ssend.at[n],
            recv_sem=srecv.at[n], device_id=target, device_id_type=MESH,
        )
        return n, q, t

    def widened(n, k):
        scale = ins[n, pl.ds(k, 1), :] * (1.0 / 65534.0)
        return (inq[n * CHUNK + k].astype(jnp.int32).astype(jnp.float32) + 32767.0) * scale

    for g, s in order:
        way, kind, chunks = groups[g]
        step, begin, size = chunks[s]
        a, b = loads[g, s]
        a.wait()
        b.wait_recv()
        if kind == "mine":

            def add(k, _, step=step, begin=begin):
                own[step, begin + k] += sib[step, begin + k]
                return 0

            lax.fori_loop(0, size, add, 0)
            continue
        joined = None
        if kind == "join":
            joined, q, t = message(way, "far", s)
            q.wait_recv()
            t.wait_recv()
        n, q, t = message(way, kind, s)

        def pack(k, _, step=step, begin=begin, joined=joined, n=n):
            total = own[step, begin + k] + sib[step, begin + k]
            if joined is not None:
                total += widened(joined, k)
            top = jnp.max(total, axis=0, keepdims=True)
            outs[n, pl.ds(k, 1), :] = top
            scaled = total * (65534.0 / jnp.maximum(top, 1e-30)) - 32767.0
            outq[n * CHUNK + k] = jnp.round(scaled).astype(jnp.int32).astype(jnp.int16)
            return 0

        lax.fori_loop(0, size, pack, 0)
        q.start()
        t.start()
        sends.append((q, t))

    for kind in ("near", "join"):
        for s in range(steps):
            for way in (0, 1):
                n, q, t = message(way, kind, s)
                q.wait_recv()
                t.wait_recv()
                begin = half * ((kind == "near") ^ (way == 1)) + s * CHUNK

                def finish(k, _, begin=begin, n=n):
                    own[0, begin + k] += widened(n, k)
                    return 0

                lax.fori_loop(0, CHUNK, finish, 0)
    done = pltpu.make_async_copy(own.at[0], out, lsem.at[0])
    done.start()
    for q, t in sends:
        q.wait_send()
        t.wait_send()
    for g, s in order:
        loads[g, s][1].wait_send()
    done.wait()


def reduce(ny, part):
    pairs, tile = part.shape[1], part.shape[2]
    quarter = pairs // 4
    n = 2 * 3 * (quarter // 2 // CHUNK)
    m = 8 * (quarter // 2 // CHUNK)
    dma = pltpu.SemaphoreType.DMA
    return pl.pallas_call(
        functools.partial(reduce_kernel, ny, quarter),
        name="ring_reduce",
        out_shape=jax.ShapeDtypeStruct((quarter, tile, tile), jnp.float32),
        in_specs=[pl.BlockSpec(memory_space=pl.ANY)],
        out_specs=pl.BlockSpec(memory_space=pl.ANY),
        scratch_shapes=[
            pltpu.VMEM((4, quarter, tile, tile), jnp.float32),
            pltpu.VMEM((4, quarter, tile, tile), jnp.float32),
            pltpu.VMEM((n * CHUNK, tile, tile), jnp.int16),
            pltpu.VMEM((n, 8, tile), jnp.float32),
            pltpu.VMEM((n * CHUNK, tile, tile), jnp.int16),
            pltpu.VMEM((n, 8, tile), jnp.float32),
            dma((m,)), dma((m,)), dma((m,)), dma((n,)), dma((n,)), dma((n,)), dma((n,)),
        ],
        compiler_params=pltpu.CompilerParams(collective_id=1, has_side_effects=True),
    )(part)


def local(
    ny,
    eval_tiles,
    eval_tile_list,
    corpus_tiles,
    corpus_tile_list,
    pair_eval_block,
    pair_corpus_block,
    pair_count,
    eval_norm,
    corpus_norm,
):
    slices = lax.axis_size("vocab")
    docs, slots, tile_rows, term_width = corpus_tiles.shape
    tiles_slice = VOCAB // (term_width * slices)
    pairs = pair_eval_block.shape[0]
    quarter = pairs // slices
    rows = slots * tile_rows
    used = 2 * pairs + docs * slots + 1
    meta = jnp.concatenate(
        [
            pair_eval_block,
            pair_corpus_block,
            corpus_tile_list.reshape(-1),
            pair_count,
            jnp.zeros((-used % 1024,), jnp.int32),
        ]
    ).reshape(-1, 128)
    eval_in = eval_tiles.reshape(rows, term_width)
    corpus_in = corpus_tiles.reshape(docs * rows, term_width)
    rows_a = rows * 7 // 24
    gath, pcorpus, _, pmeta = gather(ny, rows_a, eval_in, corpus_in, meta)
    part = partial_dots(
        pairs, docs, slots, tiles_slice, meta, pmeta, eval_tile_list.T, gath, corpus_in, pcorpus
    )
    summed = reduce(ny, part)
    position = jnp.arange(pairs, dtype=jnp.int32)
    own_live = position < pair_count[0]
    first_pair = lax.axis_index("vocab") * quarter
    mine_eval = lax.dynamic_slice_in_dim(pair_eval_block, first_pair, quarter)
    mine_block = lax.dynamic_slice_in_dim(pair_corpus_block, first_pair, quarter)
    mine_live = lax.dynamic_slice_in_dim(own_live, first_pair, quarter)
    eval_scale = eval_norm.reshape(-1, tile_rows)[mine_eval]
    corpus_scale = corpus_norm.reshape(-1, tile_rows)[mine_block]
    cosine = summed / (eval_scale[:, :, None] * corpus_scale[:, None, :])
    return jnp.where(mine_live[:, None, None], cosine, 0.0)


def solution(mesh):
    ny = mesh.shape["corpus"] // (2 * NZ)
    in_specs = (
        P("corpus", "vocab", None, None),
        P(None, "vocab"),
        P("corpus", "vocab", None, None),
        P("corpus", "vocab"),
        P("corpus"),
        P("corpus"),
        P("corpus"),
        P(),
        P("corpus"),
    )
    out_specs = P(("corpus", "vocab"), None, None)
    return jax.shard_map(
        functools.partial(local, ny), mesh=mesh, in_specs=in_specs, out_specs=out_specs, check_vma=False
    )
```

time: 637 us -> 157 us (0.25)
  waiting for transfers between devices: 551 us -> 0 us
  Pallas kernels: 0 us -> 149 us
  local copies, waits for them, and re-layouts: 34.3 us -> 3.34 us
  matrix products: 14 us -> 0 us
  between operations: 14.1 us -> 0.76 us
  other arithmetic: 12.8 us -> 3.16 us
  loops' own time: 8.9 us -> 0 us
    all_gather x1 -> x0, waiting for transfers between devices: 276 us -> none  [local(): every_eval = lax.all_gather(eval_tiles, 'corpus', axis=0, tiled=True)]
    reduce_scatter x1 -> x0, waiting for transfers between devices: 274 us -> none  [local(): lax.psum_scatter(lax.fori_loop(0, groups, one_group, start_totals), 'voca...]
    pallas_call x0 -> x3, Pallas kernels: none -> 149 us  [the longest x1 78.3 us: gather(): pl.pallas_call(functools.partial(gather_kernel, ny, rows_a), name='plane_...]
    gather x8 -> x0, local copies, waits for them, and re-layouts: 28.3 us -> none  [the longest x2 21.1 us: compute(): eval_part = every_eval[eval_index]]
    dot_general x4 -> x0, matrix products: 14 us -> none  [the longest x2 9.85 us: compute(): jnp.einsum('gij,gjrt->girt', matched.astype(jnp.bfloat16), corpus_part, p...]
    reduce_or x12 -> x0, other arithmetic: 9.43 us -> none  [one_group(): return lax.cond(jnp.any(living), compute, lambda current: current, totals)]
    another operation x13 -> x0, loops' own time: 8.9 us -> none  [the longest x1 8.64 us: local(): lax.fori_loop(0, groups, one_group, start_totals)]
  transfers between devices with their start and end apart: 2 -> 0, of which waited for: 2 -> 0; matrix products, arithmetic and copies ran while one was open for 0% -> 0% of each run, Pallas kernels for 0% -> 0%
where the time goes in v1:
time: 157 us; the launch traced here: 156 us
  Pallas kernels  149 us (95%)
  local copies, waits for them, and re-layouts  3.34 us (2%)
  other arithmetic  3.16 us (2%)
    pallas_call x1, Pallas kernels, gather(): pl.pallas_call(functools.partial(gather_kernel, ny, rows_a), name='plane_...  78.3 us
    pallas_call x1, Pallas kernels, reduce(): pl.pallas_call(functools.partial(reduce_kernel, ny, quarter), name='ring_...  43.5 us
    pallas_call x1, Pallas kernels, partial_dots(): pl.pallas_call(functools.partial(dot_kernel, pairs, docs, slots, tiles_sl...  27.1 us

profile of v1, /device:TPU:33, one launch (start us, length us, event | category | flops | bytes accessed | tf_op | source)
XLA Modules:
  0.0 156.2 jit_solution(8560609272944341706)
XLA Ops:
  0.0 0.0 copy-start
  0.7 0.8 reshape.21
  1.4 1.3 concatenate.3
  2.8 78.3 %plane_gather.1 = (bf16[32,384,512]{2,1,0:T(8,128)(2,1)}, bf16[1536,512]{1,0:T(8,128)(2,1)}, bf16[1536,512]{1,0:T(8,128)(2,1)}, s32[8,128]{1,0:T(8,128)}) custom-call(bf16[384,512]{1,0:T(8,128)(2,1)} %bitcast.12, bf16[1536,512]{1,0:T(8,128)(2,1)} %bitcast.9, s32[8,128]{1,0:T(8,128)} %bitcast.13), custom_call_target="tpu_custom_call" | custom-call | tf_op jit(solution)/shard_map/plane_gather/pallas_call | solution.py:179
  81.1 27.1 %partial_dots.1.part = f32[2,96,128,128]{3,2,1,0:T(8,128)} custom-call(s32[8,128]{1,0:T(8,128)} %bitcast.14, s32[8,128]{1,0:T(8,128)} %get-tuple-element.8.pmeta, s32[3,64]{1,0:T(4,128)} %bitcast.15, bf16[32,384,512]{2,1,0:T(8,128)(2,1)} %get-tuple-element.9.gath, bf16[1536,512]{1,0:T(8,128)(2,1)} %bitcast.10, bf16[1536,512]{1,0:T(8,128)(2,1)} %get-tuple-element.10.pcorpus), custom_call_target="tpu_custom_call" | custom-call | tf_op jit(solution)/shard_map/partial_dots/pallas_call | solution.py:291
  108.2 0.0 copy-start.2
  108.2 0.0 copy-start.3
  108.2 0.0 copy-start.1
  108.2 43.5 %ring_reduce.1 = f32[24,128,128]{2,1,0:T(8,128)} custom-call(f32[2,96,128,128]{3,2,1,0:T(8,128)} %partial_dots.1.part), custom_call_target="tpu_custom_call" | custom-call | tf_op jit(solution)/shard_map/ring_reduce/pallas_call | solution.py:448
  151.8 0.0 copy-done.2
  151.8 0.0 copy-done.3
  151.8 0.1 compare_select_fusion
  151.9 0.0 copy-done
  151.9 0.6 gather_fusion
  152.5 0.0 copy-done.1
  152.5 0.6 gather_fusion.1
  153.1 0.1 dynamic_slice.9
  153.2 3.1 %divide_select_fusion = f32[24,128,128]{2,1,0:T(8,128)} fusion(f32[24,128,128]{2,1,0:T(8,128)} %ring_reduce.1, f32[24,128]{1,0:T(8,128)S(1)} %gather_fusion.1, f32[24,128]{1,0:T(8,128)S(1)} %gather_fusion, pred[24]{0:T(512)(128)(4,1)S(1)} %dynamic_slice.9), kind=kLoop, calls=%fused_computation.2 | loop fusion | flops 1179648 | bytes 3170328 | tf_op jit(solution)/shard_map/jit(_where)/select_n | solution.py:512
  (4 shorter events, 0.0 us)
Async XLA Ops:
  0.0 151.9 %copy-start = (f32[8192]{0:T(1024)S(1)}, f32[8192]{0:T(1024)}, u32[]{:S(2)}) copy-start(f32[8192]{0:T(1024)} %param.16) | copy-start | bytes 98308
  108.2 43.6 %copy-start.2 = (s32[96]{0:T(128)S(1)}, s32[96]{0:T(128)}, u32[]{:S(2)}) copy-start(s32[96]{0:T(128)} %param.13) | copy-start | bytes 1156
  108.2 43.6 %copy-start.3 = (s32[96]{0:T(128)S(1)}, s32[96]{0:T(128)}, u32[]{:S(2)}) copy-start(s32[96]{0:T(128)} %param.14) | copy-start | bytes 1156
  108.2 44.2 %copy-start.1 = (f32[512]{0:T(512)S(1)}, f32[512]{0:T(512)}, u32[]{:S(2)}) copy-start(f32[512]{0:T(512)} %param.17) | copy-start | bytes 6148
